TPU v7x, 256 devices: a whole 4x4x8 slice. The times are simulated.
256 devices in a mesh: grp: 8 (over x, z_lo), ref: 32 (over z_hi, y, core).
Axes of the slice: x: 4, y: 4, z: 8 (z_hi: 4, z_lo: 2; z = z_hi * 2 + z_lo), core: 2. Of those that a mesh axis runs over, the one named last changes fastest.
Arguments:
- particles: bfloat16 [2048, 512], P(('grp', 'ref')), may hold values from -30 to 30
- samples: bfloat16 [131072, 512], P('ref'), may hold values from -6 to 6
Outputs:
- moved: float32 [2048, 512], P(('grp', 'ref'))
All inputs are finite; a program needn't handle non-finite values.
Results may differ from a plain program's by a relative error of at most 0.0035.
Values may be sent and summed in bfloat16 or wider, within the bound.
A program may use at most 128 MiB of HBM per device.

v0:
```python
import jax
import jax.numpy as jnp
from jax import lax
from jax.sharding import PartitionSpec as P

KERNEL_WIDTH = 16


step_size = 8.0
masked_score = -1e30


def combined_all(part, axis, combine):
    gathered = jax.tree.map(lambda a: lax.all_gather(a, axis), part)

    def take(source):
        return jax.tree.map(lambda a: lax.dynamic_index_in_dim(a, source, 0, False), gathered)

    return lax.fori_loop(
        1, lax.axis_size(axis), lambda source, state: combine(state, take(source)), take(0)
    )


def square_norms(values):
    wide = values.astype(jnp.float32)
    return jnp.sum(wide * wide, axis=1)


def row_terms(row_block, row_sq, row_ids, samples, ref_sq, columns, column_sq, column_ids):
    cross_scores = (
        2.0 * jnp.einsum("rd,md->rm", row_block, samples, preferred_element_type=jnp.float32)
        - row_sq[:, None]
        - ref_sq[None, :]
    ) / (2.0 * KERNEL_WIDTH)
    cross_max = jnp.max(cross_scores, axis=1)
    cross_weights = jnp.exp(cross_scores - cross_max[:, None])
    cross_total = jnp.sum(cross_weights, axis=1)
    cross_sum = jnp.dot(
        cross_weights.astype(jnp.bfloat16), samples, preferred_element_type=jnp.float32
    )
    self_scores = (
        2.0 * jnp.einsum("rd,cd->rc", row_block, columns, preferred_element_type=jnp.float32)
        - row_sq[:, None]
        - column_sq[None, :]
    ) / (2.0 * KERNEL_WIDTH)
    diag_mask = row_ids[:, None] == column_ids[None, :]
    self_scores = jnp.where(diag_mask, masked_score, self_scores)
    self_max = jnp.max(self_scores, axis=1)
    self_weights = jnp.where(diag_mask, 0.0, jnp.exp(self_scores - self_max[:, None]))
    self_total = jnp.sum(self_weights, axis=1)
    self_sum = jnp.dot(
        self_weights.astype(jnp.bfloat16), columns, preferred_element_type=jnp.float32
    )
    return (cross_max, cross_total, cross_sum, self_max, self_total, self_sum)


def combine_parts(left_side, right_side):
    cross_top = jnp.maximum(left_side[0], right_side[0])
    left_cross = jnp.exp(left_side[0] - cross_top)
    right_cross = jnp.exp(right_side[0] - cross_top)
    self_top = jnp.maximum(left_side[3], right_side[3])
    left_self = jnp.exp(left_side[3] - self_top)
    right_self = jnp.exp(right_side[3] - self_top)
    return (
        cross_top,
        left_side[1] * left_cross + right_side[1] * right_cross,
        left_side[2] * left_cross[:, None] + right_side[2] * right_cross[:, None],
        self_top,
        left_side[4] * left_self + right_side[4] * right_self,
        left_side[5] * left_self[:, None] + right_side[5] * right_self[:, None],
    )


def per_device(particles, samples):
    part_dev = particles.shape[0]
    grp_count = lax.axis_size("grp")
    grp_pos = lax.axis_index("grp")
    ref_pos = lax.axis_index("ref")
    group = lax.all_gather(particles, "ref", axis=0, tiled=True)
    columns = lax.all_gather(particles, "grp", axis=0, tiled=True)
    group_rows = group.shape[0]
    column_ids = (
        jnp.arange(grp_count, dtype=jnp.int32)[:, None] * group_rows
        + ref_pos * part_dev
        + jnp.arange(part_dev, dtype=jnp.int32)[None, :]
    ).reshape(-1)
    row_ids = grp_pos * group_rows + jnp.arange(group_rows, dtype=jnp.int32)
    group_sq = square_norms(group)
    column_sq = square_norms(columns)
    ref_sq = square_norms(samples)
    block_rows = min(512, group_rows)
    blocks = group_rows // block_rows

    def one_block(inputs):
        row_block, row_sq, block_ids = inputs
        return row_terms(
            row_block, row_sq, block_ids, samples, ref_sq, columns, column_sq, column_ids
        )

    stacked_terms = lax.map(
        one_block,
        (
            group.reshape(blocks, block_rows, group.shape[1]),
            group_sq.reshape(blocks, block_rows),
            row_ids.reshape(blocks, block_rows),
        ),
    )
    cross_max, cross_total, cross_sum, self_max, self_total, self_sum = tuple(
        (stacked.reshape((group_rows,) + stacked.shape[2:]) for stacked in stacked_terms)
    )
    merged = combined_all(
        (cross_max, cross_total, cross_sum, self_max, self_total, self_sum), "ref", combine_parts
    )
    start = ref_pos * part_dev
    cross_mean = (
        lax.dynamic_slice_in_dim(merged[2], start, part_dev, 0)
        / lax.dynamic_slice_in_dim(merged[1], start, part_dev, 0)[:, None]
    )
    self_mean = (
        lax.dynamic_slice_in_dim(merged[5], start, part_dev, 0)
        / lax.dynamic_slice_in_dim(merged[4], start, part_dev, 0)[:, None]
    )
    return particles.astype(jnp.float32) + step_size * (cross_mean - self_mean)


def solution(mesh):
    in_specs = (P(("grp", "ref"), None), P("ref", None))
    out_specs = P(("grp", "ref"), None)
    return jax.shard_map(
        per_device, mesh=mesh, in_specs=in_specs, out_specs=out_specs, check_vma=False
    )
```

profile of v0, /device:TPU:2, one launch (start us, length us, event | category | flops | bytes accessed | tf_op | source)
XLA Modules:
  0.0 376.5 jit_solution(6727869570558348518)
XLA Ops:
  6.5 28.0 %all_gather.28 = bf16[64,512]{1,0:T(8,128)(2,1)S(1)} all-gather(bf16[8,512]{1,0:T(8,128)(2,1)} %param.4), channel_id=1, replica_groups=mesh['grp'=8,'ref'=32] {'grp'}, dimensions={0}, use_global_device_ids=true | all-gather | bytes 73728 | tf_op jit(solution)/shard_map/all_gather | solution.py:80
  34.5 46.8 %all_gather.24 = bf16[256,512]{1,0:T(8,128)(2,1)S(1)} all-gather(bf16[8,512]{1,0:T(8,128)(2,1)} %param.4), channel_id=1, replica_groups=mesh['grp'=8,'ref'=32] {'ref'}, dimensions={0}, use_global_device_ids=true | all-gather | bytes 270336 | tf_op jit(solution)/shard_map/all_gather | solution.py:79
  83.2 3.2 multiply_reduce_fusion
  88.1 2.0 copy-done.1
  90.2 2.1 fusion.7
  92.4 40.9 %all-gather.9 = f32[32,1,256]{2,1,0:T(1,128)S(1)} all-gather(f32[1,1,256]{2,1,0:T(1,128)S(1)} %bitcast.65), channel_id=6, replica_groups=mesh['grp'=8,'ref'=32] {'ref'}, dimensions={0}, use_global_device_ids=true | all-gather | bytes 33792 | tf_op jit(solution)/shard_map/all_gather | solution.py:14
  133.3 44.0 %all-gather.8 = f32[32,1,256]{2,1,0:T(1,128)S(1)} all-gather(f32[1,1,256]{2,1,0:T(1,128)S(1)} %bitcast.64), channel_id=5, replica_groups=mesh['grp'=8,'ref'=32] {'ref'}, dimensions={0}, use_global_device_ids=true | all-gather | bytes 33792 | tf_op jit(solution)/shard_map/all_gather | solution.py:14
  177.3 3.1 fusion.6
  180.4 39.5 %all-gather.7 = f32[32,1,256]{2,1,0:T(1,128)S(1)} all-gather(f32[1,1,256]{2,1,0:T(1,128)S(1)} %bitcast.67), channel_id=3, replica_groups=mesh['grp'=8,'ref'=32] {'ref'}, dimensions={0}, use_global_device_ids=true | all-gather | bytes 33792 | tf_op jit(solution)/shard_map/all_gather | solution.py:14
  219.9 40.3 %all-gather.6 = f32[32,1,256]{2,1,0:T(1,128)S(1)} all-gather(f32[1,1,256]{2,1,0:T(1,128)S(1)} %bitcast.66), channel_id=2, replica_groups=mesh['grp'=8,'ref'=32] {'ref'}, dimensions={0}, use_global_device_ids=true | all-gather | bytes 33792 | tf_op jit(solution)/shard_map/all_gather | solution.py:14
  261.3 56.3 %all-gather.13.cloned.1.call-done = f32[8192,512]{1,0:T(8,128)} async-done(((f32[256,512]{1,0:T(8,128)}), f32[8192,512]{1,0:T(8,128)}) %all-gather.13.cloned.1.call-update) | async-done | bytes 16777232 | tf_op jit(solution)/shard_map/all_gather | solution.py:14
  318.8 50.0 %while.6 = (s32[]{:T(128)}, f32[256]{0:T(256)S(1)}, f32[256]{0:T(256)S(1)}, f32[256,512]{1,0:T(8,128)S(1)}, f32[256]{0:T(256)S(1)}, /*index=5*/f32[256]{0:T(256)...) while((s32[]{:T(128)}, f32[256]{0:T(256)S(1)}, ...), condition=%wide.region_8.9_spmd, body=%wide.region_7.8_spmd.sunk | while | flops 789509 | bytes 3174603 | solution.py:19
  320.5 1.5 fusion.32
  322.1 1.5 fusion.32
  323.7 1.5 fusion.32
  325.3 1.5 fusion.32
  328.6 1.5 fusion.32
  331.8 1.5 fusion.32
  333.4 1.5 fusion.32
  335.0 1.5 fusion.32
  336.6 1.5 fusion.32
  339.9 1.5 fusion.32
  343.1 1.5 fusion.32
  344.7 1.5 fusion.32
  346.3 1.5 fusion.32
  347.9 1.5 fusion.32
  349.6 1.5 fusion.32
  351.2 1.5 fusion.32
  354.4 1.5 fusion.32
  357.6 1.5 fusion.32
  359.2 1.5 fusion.32
  360.8 1.5 fusion.32
  (230 shorter events, 25.4 us)
Async XLA Ops:
  6.5 253.7 %all-gather.15.cloned.1.call-start = ((), (), s32[]{:S(2)}) async-start(), calls=%async_computation.1 | async-start | bytes 17301504 | tf_op jit(solution)/shard_map/all_gather | solution.py:14
  83.2 234.5 %all-gather.13.cloned.1.call-start = ((), (), s32[]{:S(2)}) async-start(), calls=%async_computation | async-start | bytes 17301504 | tf_op jit(solution)/shard_map/all_gather | solution.py:14
  83.2 3.5 copy-start
  88.1 2.1 copy-start.1
  318.7 50.2 %copy-start.2 = (bf16[8,512]{1,0:T(8,128)(2,1)S(1)}, bf16[8,512]{1,0:T(8,128)(2,1)}, u32[]{:S(2)}) copy-start(bf16[8,512]{1,0:T(8,128)(2,1)} %param.4) | copy-start | bytes 24580
Sparse Core Ops, SparseCore 0:
  83.3 114.8 all-gather.14
  200.7 116.8 all-gather.12
where the time goes:
time: 378 us; the launch traced here: 376 us
  blocking collectives  240 us (63%)
  waiting for transfers between devices  56.4 us (15%)
  other arithmetic  54.2 us (14%)
  between operations  13.5 us (4%)
  local copies, waits for them, and re-layouts  6.1 us (2%)
  matrix products  4.9 us (1%)
    all_gather x4, blocking collectives, combined_all(): gathered = jax.tree.map(lambda a: lax.all_gather(a, axis), part)  165 us
    all_gather x2, waiting for transfers between devices, combined_all(): gathered = jax.tree.map(lambda a: lax.all_gather(a, axis), part)  56.3 us
    all_gather x1, blocking collectives, per_device(): group = lax.all_gather(particles, 'ref', axis=0, tiled=True)  46.8 us
    add x31, other arithmetic, combine_parts(): left_side[5] * left_self[:, None] + right_side[5] * right_self[:, None]  45.5 us
    all_gather x1, blocking collectives, per_device(): columns = lax.all_gather(particles, 'grp', axis=0, tiled=True)  28 us
  transfers between devices with their start and end apart: 2, of which 1 were waited for; matrix products, arithmetic and copies ran while one was open for 3% of the time, Pallas kernels for 0%

commit v1 on v0

v1 whole, which is shorter than its diff:
```python
import functools
import math

import jax
import jax.numpy as jnp
from jax import lax
from jax.experimental import pallas as pl
from jax.experimental.pallas import tpu as pltpu
from jax.sharding import PartitionSpec as P

KERNEL_WIDTH = 16
STEP_SIZE = 8.0
MASKED = -1e30
SCALE = math.log2(math.e) / (2.0 * KERNEL_WIDTH)
MESH = pl.DeviceIdType.MESH
CHUNK = 512
LANES = 128


def split3(value):
    hi = value.astype(jnp.bfloat16).astype(jnp.float32)
    mid = (value - hi).astype(jnp.bfloat16).astype(jnp.float32)
    return hi, mid, value - hi - mid


def with_stats(total, top, mass):
    lane = lax.broadcasted_iota(jnp.int32, (total.shape[0], LANES), 1)
    stats = jnp.zeros((total.shape[0], LANES), jnp.float32)
    for at, piece in enumerate(split3(top) + split3(mass)):
        stats = jnp.where(lane == at, piece, stats)
    return jnp.concatenate([total, stats], axis=1)


def merged_mean(parts):
    wide = parts.astype(jnp.float32)
    d = wide.shape[2] - LANES
    top = wide[:, :, d : d + 1] + wide[:, :, d + 1 : d + 2] + wide[:, :, d + 2 : d + 3]
    mass = wide[:, :, d + 3 : d + 4] + wide[:, :, d + 4 : d + 5] + wide[:, :, d + 5 : d + 6]
    share = jnp.exp2(top - jnp.max(top, axis=0, keepdims=True))
    return jnp.sum(share * wide[:, :, :d], axis=0) / jnp.sum(share * mass, axis=0)


def lane_square_norms(values):
    n, d = values.shape
    wide = values.astype(jnp.float32)
    wide = wide * wide
    part = wide[:, :LANES]
    for at in range(LANES, d, LANES):
        part = part + wide[:, at : at + LANES]
    return jnp.sum(part.T, axis=0, keepdims=True)


def kernel(
    p_ref, samples_ref, out_ref,
    smp, rows, cols, pmat, ref_sq, scores, acc, send_c, recv_c, send_s, recv_s,
    load_sem, gs_sem, gr_sem, cs_sem, cr_sem, ss_sem, sr_sem,
):
    n_ref, n_grp = lax.axis_size("ref"), lax.axis_size("grp")
    me, mine = lax.axis_index("ref"), lax.axis_index("grp")
    part, d = p_ref.shape
    n_rows = n_ref * part
    chunks = smp.shape[0]

    def load(j):
        return pltpu.make_async_copy(
            samples_ref.at[pl.ds(j * CHUNK, CHUNK)], smp.at[j], load_sem.at[j]
        )

    for j in range(chunks):
        load(j).start()

    barrier = pltpu.get_barrier_semaphore()

    def greet_ref(k, c):
        pl.semaphore_signal(barrier, inc=1, device_id={"ref": lax.rem(me + k, n_ref)}, device_id_type=MESH)
        return c

    def greet_grp(k, c):
        pl.semaphore_signal(barrier, inc=1, device_id={"grp": lax.rem(mine + k, n_grp)}, device_id_type=MESH)
        return c

    lax.fori_loop(1, n_ref, greet_ref, 0)
    lax.fori_loop(1, n_grp, greet_grp, 0)
    rows[me] = p_ref[...]
    cols[mine] = p_ref[...]

    def square(j, c):
        load(j).wait()
        ref_sq[j] = lane_square_norms(smp[j]) * SCALE
        return c

    lax.fori_loop(0, chunks, square, 0)
    pl.semaphore_wait(barrier, n_ref - 1 + n_grp - 1)

    def give_row(k, c):
        pltpu.make_async_remote_copy(
            p_ref, rows.at[me], gs_sem.at[0], gr_sem.at[0],
            device_id={"ref": lax.rem(me + k, n_ref)}, device_id_type=MESH,
        ).start()
        return c

    def give_col(k, c):
        pltpu.make_async_remote_copy(
            p_ref, cols.at[mine], gs_sem.at[1], gr_sem.at[1],
            device_id={"grp": lax.rem(mine + k, n_grp)}, device_id_type=MESH,
        ).start()
        return c

    lax.fori_loop(1, n_ref, give_row, 0)
    lax.fori_loop(1, n_grp, give_col, 0)

    def all_of(buf, n, send_sem, recv_sem):
        return pltpu.make_async_remote_copy(
            buf.at[pl.ds(0, n - 1)], buf.at[pl.ds(0, n - 1)], send_sem, recv_sem,
            device_id={"ref": lax.rem(me + 1, n_ref)}, device_id_type=MESH,
        )

    got_rows = all_of(rows, n_ref, gs_sem.at[0], gr_sem.at[0])
    got_cols = all_of(cols, n_grp, gs_sem.at[1], gr_sem.at[1])
    got_rows.wait_recv()
    wide = rows[...].astype(jnp.float32).reshape(n_rows, d)
    pmat[...] = wide.astype(jnp.bfloat16)
    row_sq = jnp.sum(wide * wide, axis=1, keepdims=True) * SCALE

    got_cols.wait_recv()
    cmat = cols[...].astype(jnp.float32).reshape(n_grp * part, d).astype(jnp.bfloat16)
    col_sq = lane_square_norms(cmat) * SCALE
    n_cols = n_grp * part
    s = lax.dot_general(pmat[...], cmat, (((1,), (1,)), ((), ())), preferred_element_type=jnp.float32)
    s = s * (2.0 * SCALE) - col_sq
    row_id = mine * n_rows + lax.broadcasted_iota(jnp.int32, (n_rows, n_cols), 0)
    at = lax.broadcasted_iota(jnp.int32, (n_rows, n_cols), 1)
    col_id = (at // part) * n_rows + me * part + at % part
    same = row_id == col_id
    s = jnp.where(same, MASKED, s)
    s_top = jnp.max(s, axis=1, keepdims=True)
    w = jnp.where(same, 0.0, jnp.exp2(s - s_top))
    s_mass = jnp.sum(w, axis=1, keepdims=True)
    s_sum = jnp.dot(w.astype(jnp.bfloat16), cmat, preferred_element_type=jnp.float32)
    send_s[...] = with_stats(s_sum, s_top - row_sq, s_mass).reshape(n_ref, part, d + LANES).astype(jnp.bfloat16)

    def give(send, recv, send_sem, recv_sem):
        def one(k, c):
            peer = lax.rem(me + k, n_ref)
            pltpu.make_async_remote_copy(
                send.at[peer], recv.at[me], send_sem, recv_sem,
                device_id={"ref": peer}, device_id_type=MESH,
            ).start()
            return c

        lax.fori_loop(1, n_ref, one, 0)
        recv[me] = send[me]

    give(send_s, recv_s, ss_sem, sr_sem)

    def score(j, top):
        s = lax.dot_general(
            pmat[...], smp[j], (((1,), (1,)), ((), ())), preferred_element_type=jnp.float32
        )
        s = s * (2.0 * SCALE) - ref_sq[j]
        scores[j] = s
        for a in range(0, CHUNK, LANES):
            top = jnp.maximum(top, s[:, a : a + LANES])
        return top

    top = lax.fori_loop(0, chunks, score, jnp.full((n_rows, LANES), -jnp.inf, jnp.float32))
    top = jnp.max(top, axis=1, keepdims=True)
    acc[...] = jnp.zeros_like(acc)

    def weigh(j, mass):
        w = jnp.exp2(scores[j] - top)
        for a in range(0, CHUNK, LANES):
            mass = mass + w[:, a : a + LANES]
        acc[...] += jnp.dot(w.astype(jnp.bfloat16), smp[j], preferred_element_type=jnp.float32)
        return mass

    mass = lax.fori_loop(0, chunks, weigh, jnp.zeros((n_rows, LANES), jnp.float32))
    mass = jnp.sum(mass, axis=1, keepdims=True)
    send_c[...] = with_stats(acc[...], top - row_sq, mass).reshape(n_ref, part, d + LANES).astype(jnp.bfloat16)
    give(send_c, recv_c, cs_sem, cr_sem)

    got_s = all_of(recv_s, n_ref, ss_sem, sr_sem)
    got_c = all_of(recv_c, n_ref, cs_sem, cr_sem)
    got_s.wait_recv()
    self_mean = merged_mean(recv_s[...])
    got_c.wait_recv()
    cross_mean = merged_mean(recv_c[...])
    out_ref[...] = p_ref[...].astype(jnp.float32) + STEP_SIZE * (cross_mean - self_mean)
    got_rows.wait_send()
    got_cols.wait_send()
    got_s.wait_send()
    got_c.wait_send()


def per_device(n_ref, n_grp, particles, samples):
    part, d = particles.shape
    refs = samples.shape[0]
    n_rows, chunks = n_ref * part, refs // CHUNK
    dma = pltpu.SemaphoreType.DMA
    bf16, f32 = jnp.bfloat16, jnp.float32
    return pl.pallas_call(
        kernel,
        out_shape=jax.ShapeDtypeStruct((part, d), f32),
        in_specs=[pl.BlockSpec(memory_space=pltpu.VMEM), pl.BlockSpec(memory_space=pl.ANY)],
        out_specs=pl.BlockSpec(memory_space=pltpu.VMEM),
        scratch_shapes=[
            pltpu.VMEM((chunks, CHUNK, d), bf16),
            pltpu.VMEM((n_ref, part, d), bf16),
            pltpu.VMEM((n_grp, part, d), bf16),
            pltpu.VMEM((n_rows, d), bf16),
            pltpu.VMEM((chunks, 1, CHUNK), f32),
            pltpu.VMEM((chunks, n_rows, CHUNK), f32),
            pltpu.VMEM((n_rows, d), f32),
            pltpu.VMEM((n_ref, part, d + LANES), bf16),
            pltpu.VMEM((n_ref, part, d + LANES), bf16),
            pltpu.VMEM((n_ref, part, d + LANES), bf16),
            pltpu.VMEM((n_ref, part, d + LANES), bf16),
            dma((chunks,)), dma((2,)), dma((2,)), dma, dma, dma, dma,
        ],
        compiler_params=pltpu.CompilerParams(
            collective_id=0, has_side_effects=True, vmem_limit_bytes=56 * 2**20
        ),
        name="mmd_step",
    )(particles, samples)


def solution(mesh):
    step = functools.partial(per_device, mesh.shape["ref"], mesh.shape["grp"])
    return jax.shard_map(
        step,
        mesh=mesh,
        in_specs=(P(("grp", "ref"), None), P("ref", None)),
        out_specs=P(("grp", "ref"), None),
        check_vma=False,
    )
```

time: 378 us -> 40.7 us (0.11)
  the two profiles are of different devices: /device:TPU:2 before, /device:TPU:1 now
where the time goes in v1:
time: 40.7 us; the launch traced here: 40.4 us
  Pallas kernels  39.1 us (96%)
  local copies, waits for them, and re-layouts  1.32 us (3%)
    pallas_call x1, Pallas kernels, per_device(): pl.pallas_call(kernel, out_shape=jax.ShapeDtypeStruct((part, d), f32), in...  39.1 us
    unnamed x1, local copies, waits for them, and re-layouts  1.32 us

profile of v1, /device:TPU:1, one launch (start us, length us, event | category | flops | bytes accessed | tf_op | source)
XLA Modules:
  0.0 40.4 jit_solution(12744358858537507224)
XLA Ops:
  0.0 39.1 %mmd_step.1 = f32[8,512]{1,0:T(8,128)} custom-call(bf16[8,512]{1,0:T(8,128)(2,1)} %p_ref.1, bf16[4096,512]{1,0:T(8,128)(2,1)} %samples_ref.1), custom_call_target="tpu_custom_call" | custom-call | tf_op jit(solution)/shard_map/mmd_step/pallas_call | solution.py:201
  39.1 1.3 %copy.4 = f32[8,512]{1,0:T(8,128)} copy(f32[8,512]{1,0:T(8,128)} %mmd_step.1) | data formatting | bytes 32768

commit v2 on v1

v2 whole, which is shorter than its diff:
```python
import functools
import math

import jax
import jax.numpy as jnp
from jax import lax
from jax.experimental import pallas as pl
from jax.experimental.pallas import tpu as pltpu
from jax.sharding import PartitionSpec as P

KERNEL_WIDTH = 16
STEP_SIZE = 8.0
MASKED = -1e30
SCALE = math.log2(math.e) / (2.0 * KERNEL_WIDTH)
MESH = pl.DeviceIdType.MESH
CHUNK = 512
LANES = 128
VMEM_BYTES = 56 * 2**20
Z, Y = 4, 4


def split3(value):
    hi = value.astype(jnp.bfloat16).astype(jnp.float32)
    mid = (value - hi).astype(jnp.bfloat16).astype(jnp.float32)
    return hi, mid, value - hi - mid


def stats_lanes(*columns):
    lane = lax.broadcasted_iota(jnp.int32, (columns[0].shape[0], LANES), 1)
    stats = jnp.zeros((columns[0].shape[0], LANES), jnp.float32)
    for n, column in enumerate(columns):
        for m, piece in enumerate(split3(column)):
            stats = jnp.where(lane == 3 * n + m, piece, stats)
    return stats


def stat(stats, n):
    return stats[..., 3 * n : 3 * n + 1] + stats[..., 3 * n + 1 : 3 * n + 2] + stats[..., 3 * n + 2 : 3 * n + 3]


def merged_mean(parts, top, mass):
    share = jnp.exp2(top - jnp.max(top, axis=0, keepdims=True))
    return jnp.sum(share * parts, axis=0) / jnp.sum(share * mass, axis=0)


def lane_square_norms(values):
    n, d = values.shape
    wide = values.astype(jnp.float32)
    wide = wide * wide
    part = wide[:, :LANES]
    for at in range(LANES, d, LANES):
        part = part + wide[:, at : at + LANES]
    return jnp.sum(part.T, axis=0, keepdims=True)


def dot_nt(a, b):
    return lax.dot_general(a, b, (((1,), (1,)), ((), ())), preferred_element_type=jnp.float32)


def kernel(
    p_hbm, samples_ref, out_ref,
    p_ref, smp, rows, cols, pmat, ref_sq, scores, acc,
    send_m, recv_m, send_c, recv_c, send_s, recv_s,
    load_sem, p_sem, row_send, row_recv, col_send, col_recv, fwd_send, fwd_recv, fwc_send, fwc_recv,
    m_send, m_recv, c_send, c_recv, s_send, s_recv,
):
    n_grp = lax.axis_size("grp")
    me, mine = lax.axis_index("ref"), lax.axis_index("grp")
    core, y, zh = me % 2, (me // 2) % Y, me // (2 * Y)
    mate = me + 1 - 2 * core
    part, d = p_ref.shape
    chips = Z * Y
    half = chips * part
    chunks = smp.shape[0]
    far_first = [(a, b) for a in (2, 1, 3, 0) for b in (2, 1, 3, 0) if (a, b) != (0, 0)]

    def ahead(a, b):
        return (((zh + a) % Z) * Y + (y + b) % Y) * 2 + core

    def behind(a, b):
        return (((zh + Z - a) % Z) * Y + (y + Y - b) % Y) * 2 + core

    def remote(src, dst, send_sem, recv_sem, **where):
        return pltpu.make_async_remote_copy(
            src, dst, send_sem, recv_sem, device_id=where, device_id_type=MESH
        )

    barrier = pltpu.get_barrier_semaphore()
    for a, b in far_first:
        pl.semaphore_signal(barrier, inc=1, device_id={"ref": behind(a, b)}, device_id_type=MESH)
    for j in range(1, n_grp):
        pl.semaphore_signal(barrier, inc=1, device_id={"grp": (mine + j) % n_grp}, device_id_type=MESH)
    pl.semaphore_signal(barrier, inc=1, device_id={"ref": mate}, device_id_type=MESH)

    load_p = pltpu.make_async_copy(p_hbm, p_ref, p_sem)
    load_p.start()

    def load(j):
        return pltpu.make_async_copy(
            samples_ref.at[pl.ds(j * CHUNK, CHUNK)], smp.at[j], load_sem.at[j]
        )

    for j in range(chunks):
        load(j).start()

    load_p.wait()
    rows[0] = p_ref[...]
    cols[0] = p_ref[...]

    def square(j, c):
        load(j).wait()
        ref_sq[j] = lane_square_norms(smp[j]) * SCALE
        return c

    lax.fori_loop(0, chunks, square, 0)
    pl.semaphore_wait(barrier, chips - 1 + n_grp - 1 + 1)

    for a, b in far_first:
        remote(p_ref, rows.at[a * Y + b], row_send, row_recv.at[a], ref=ahead(a, b)).start()
    for j in range(1, n_grp):
        remote(p_ref, cols.at[j], col_send, col_recv, grp=(mine + j) % n_grp).start()

    def slots(buf, start, n, send_sem, recv_sem):
        return remote(buf.at[pl.ds(start, n)], buf.at[pl.ds(start, n)], send_sem, recv_sem, ref=mate)

    for a in (0, 1, 3, 2):
        n = Y - 1 if a == 0 else Y
        slots(rows, 0, n, row_send, row_recv.at[a]).wait_recv()
        remote(rows.at[pl.ds(a * Y, Y)], rows.at[pl.ds(chips + a * Y, Y)], fwd_send, fwd_recv, ref=mate).start()
        if a == 0:
            slots(cols, 0, n_grp - 1, col_send, col_recv).wait_recv()
            remote(cols.at[pl.ds(0, n_grp)], cols.at[pl.ds(n_grp, n_grp)], fwc_send, fwc_recv, ref=mate).start()
    forward_cols = slots(cols, n_grp, n_grp, fwc_send, fwc_recv)
    forward_cols.wait_recv()

    cwide = cols[...].astype(jnp.float32).reshape(2 * n_grp * part, d)
    cmat = cwide.astype(jnp.bfloat16)
    col_sq = lane_square_norms(cmat) * SCALE
    n_cols = 2 * n_grp * part

    forward_rows = slots(rows, chips, chips, fwd_send, fwd_recv)
    forward_rows.wait_recv()
    wide = rows[...].astype(jnp.float32).reshape(2 * half, d)
    pmat[...] = wide.astype(jnp.bfloat16)
    row_sq = jnp.sum(wide * wide, axis=1, keepdims=True) * SCALE
    center = jnp.sum(wide, axis=0, keepdims=True) * (1.0 / (2 * half))

    s = dot_nt(pmat[pl.ds(0, half), :], cmat)
    s = s * (2.0 * SCALE) - col_sq
    r = lax.broadcasted_iota(jnp.int32, (half, n_cols), 0)
    a, b = r // (Y * part), (r // part) % Y
    row_id = mine * (2 * half) + (((zh + Z - a) % Z * Y + (y + Y - b) % Y) * 2 + core) * part + r % part
    q = lax.broadcasted_iota(jnp.int32, (half, n_cols), 1)
    j = (q // part) % n_grp
    col_id = (
        (mine + n_grp - j) % n_grp * (2 * half)
        + jnp.where(q < n_grp * part, me, mate) * part
        + q % part
    )
    same = row_id == col_id
    s = jnp.where(same, MASKED, s)
    s_top = jnp.max(s, axis=1, keepdims=True)
    w = jnp.where(same, 0.0, jnp.exp2(s - s_top))
    s_mass = jnp.sum(w, axis=1, keepdims=True)
    s_sum = jnp.dot(w.astype(jnp.bfloat16), cmat, preferred_element_type=jnp.float32) - s_mass * center
    send_s[...] = s_sum.reshape(chips, part, d).astype(jnp.bfloat16)

    for a, b in far_first:
        k = a * Y + b
        remote(send_s.at[k], recv_s.at[k], s_send, s_recv, ref=behind(a, b)).start()
    recv_s[0] = send_s[0]

    top = jnp.full((2 * half, LANES), -jnp.inf, jnp.float32)
    for j in range(chunks):
        s = dot_nt(pmat[...], smp[j]) * (2.0 * SCALE) - ref_sq[j]
        scores[j] = s
        for at in range(0, CHUNK, LANES):
            top = jnp.maximum(top, s[:, at : at + LANES])
    top = jnp.max(top, axis=1, keepdims=True)
    mass = jnp.zeros((2 * half, LANES), jnp.float32)
    for j in range(chunks):
        w = jnp.exp2(scores[j] - top)
        for at in range(0, CHUNK, LANES):
            mass = mass + w[:, at : at + LANES]
        term = jnp.dot(w.astype(jnp.bfloat16), smp[j], preferred_element_type=jnp.float32)
        if j == 0:
            acc[...] = term
        else:
            acc[...] += term
    mass = jnp.sum(mass, axis=1, keepdims=True)
    total = acc[...] - mass * center
    top = top - row_sq

    send_m[:, pl.ds(0, d)] = total[half:].astype(jnp.bfloat16)
    send_m[:, pl.ds(d, LANES)] = stats_lanes(top[half:], mass[half:]).astype(jnp.bfloat16)
    swap = remote(send_m, recv_m, m_send, m_recv, ref=mate)
    swap.start()
    swap.wait_recv()
    theirs = recv_m[:, pl.ds(0, d)].astype(jnp.float32)
    stats = recv_m[:, pl.ds(d, LANES)].astype(jnp.float32)
    c_top = jnp.maximum(top[:half], stat(stats, 0))
    ours_share, their_share = jnp.exp2(top[:half] - c_top), jnp.exp2(stat(stats, 0) - c_top)
    c_mass = mass[:half] * ours_share + stat(stats, 1) * their_share
    c_sum = total[:half] * ours_share + theirs * their_share
    send_c[:, :, pl.ds(0, d)] = c_sum.reshape(chips, part, d).astype(jnp.bfloat16)
    stats = stats_lanes(c_top, c_mass, s_top - row_sq[:half], s_mass)
    send_c[:, :, pl.ds(d, LANES)] = stats.reshape(chips, part, LANES).astype(jnp.bfloat16)

    for a, b in far_first:
        k = a * Y + b
        remote(send_c.at[k], recv_c.at[k], c_send, c_recv, ref=behind(a, b)).start()
    recv_c[0] = send_c[0]

    got_s = slots(recv_s, 0, chips - 1, s_send, s_recv)
    got_c = slots(recv_c, 0, chips - 1, c_send, c_recv)
    got_s.wait_recv()
    got_c.wait_recv()
    stats = recv_c[:, :, pl.ds(d, LANES)].astype(jnp.float32)
    cross = merged_mean(recv_c[:, :, pl.ds(0, d)].astype(jnp.float32), stat(stats, 0), stat(stats, 1))
    own = merged_mean(recv_s[...].astype(jnp.float32), stat(stats, 2), stat(stats, 3))
    out_ref[...] = p_ref[...].astype(jnp.float32) + STEP_SIZE * (cross - own)
    slots(rows, 0, chips - 1, row_send, row_recv.at[0]).wait_send()
    slots(cols, 0, n_grp - 1, col_send, col_recv).wait_send()
    forward_rows.wait_send()
    forward_cols.wait_send()
    swap.wait_send()
    got_s.wait_send()
    got_c.wait_send()


def per_device(n_ref, n_grp, particles, samples):
    part, d = particles.shape
    refs = samples.shape[0]
    chips, chunks = n_ref // 2, refs // CHUNK
    n_rows, half = n_ref * part, n_ref * part // 2
    dma = pltpu.SemaphoreType.DMA
    bf16, f32 = jnp.bfloat16, jnp.float32
    return pl.pallas_call(
        kernel,
        out_shape=jax.ShapeDtypeStruct((part, d), f32),
        in_specs=[pl.BlockSpec(memory_space=pl.ANY)] * 2,
        out_specs=pl.BlockSpec(memory_space=pltpu.VMEM),
        scratch_shapes=[
            pltpu.VMEM((part, d), bf16),
            pltpu.VMEM((chunks, CHUNK, d), bf16),
            pltpu.VMEM((n_ref, part, d), bf16),
            pltpu.VMEM((2 * n_grp, part, d), bf16),
            pltpu.VMEM((n_rows, d), bf16),
            pltpu.VMEM((chunks, 1, CHUNK), f32),
            pltpu.VMEM((chunks, n_rows, CHUNK), f32),
            pltpu.VMEM((n_rows, d), f32),
            pltpu.VMEM((half, d + LANES), bf16),
            pltpu.VMEM((half, d + LANES), bf16),
            pltpu.VMEM((chips, part, d + LANES), bf16),
            pltpu.VMEM((chips, part, d + LANES), bf16),
            pltpu.VMEM((chips, part, d), bf16),
            pltpu.VMEM((chips, part, d), bf16),
            dma((chunks,)), dma, dma, dma((Z,)), dma, dma, dma, dma, dma, dma,
            dma, dma, dma, dma, dma, dma,
        ],
        compiler_params=pltpu.CompilerParams(
            collective_id=0, has_side_effects=True, vmem_limit_bytes=VMEM_BYTES
        ),
        name="mmd_step",
    )(particles, samples)


def solution(mesh):
    step = functools.partial(per_device, mesh.shape["ref"], mesh.shape["grp"])
    return jax.shard_map(
        step,
        mesh=mesh,
        in_specs=(P(("grp", "ref"), None), P("ref", None)),
        out_specs=P(("grp", "ref"), None),
        check_vma=False,
    )
```

time: 40.7 us -> 32.2 us (0.79)
  the two profiles are of different devices: /device:TPU:1 before, /device:TPU:2 now
where the time goes in v2:
time: 32.2 us; the launch traced here: 31.8 us
  Pallas kernels  30.4 us (94%)
  local copies, waits for them, and re-layouts  1.32 us (4%)
    pallas_call x1, Pallas kernels, per_device(): pl.pallas_call(kernel, out_shape=jax.ShapeDtypeStruct((part, d), f32), in...  30.4 us
    unnamed x1, local copies, waits for them, and re-layouts  1.32 us

profile of v2, /device:TPU:2, one launch (start us, length us, event | category | flops | bytes accessed | tf_op | source)
XLA Modules:
  0.0 31.8 jit_solution(16910525910064523734)
XLA Ops:
  0.0 30.4 %mmd_step.1 = f32[8,512]{1,0:T(8,128)} custom-call(bf16[8,512]{1,0:T(8,128)(2,1)} %p_hbm.1, bf16[4096,512]{1,0:T(8,128)(2,1)} %samples_ref.1), custom_call_target="tpu_custom_call" | custom-call | tf_op jit(solution)/shard_map/mmd_step/pallas_call | solution.py:238
  30.4 1.3 %copy.4 = f32[8,512]{1,0:T(8,128)} copy(f32[8,512]{1,0:T(8,128)} %mmd_step.1) | data formatting | bytes 32768

commit v3 on v2

--- a/solution.py
+++ b/solution.py
@@ -16,7 +16,7 @@
 CHUNK = 512
 LANES = 128
 VMEM_BYTES = 56 * 2**20
-Z, Y = 4, 4
+Z, Y, LO = 4, 4, 2
 
 
 def split3(value):
@@ -74,11 +74,26 @@
     chunks = smp.shape[0]
     far_first = [(a, b) for a in (2, 1, 3, 0) for b in (2, 1, 3, 0) if (a, b) != (0, 0)]
 
-    def ahead(a, b):
-        return (((zh + a) % Z) * Y + (y + b) % Y) * 2 + core
-
-    def behind(a, b):
-        return (((zh + Z - a) % Z) * Y + (y + Y - b) % Y) * 2 + core
+    lo, x = mine % LO, mine // LO
+
+    def goes_to(a, b):
+        to_lo = (lo, 0, 1 - lo, 1)[a]
+        where = {"grp": x * LO + to_lo, "ref": (((zh + a) % Z) * Y + (y + b) % Y) * 2 + core}
+        return where, (0, 1 + 2 * lo, 2, 1 + 2 * lo)[a] * Y + b
+
+    def z_of_slot(s):
+        if s == 0:
+            return zh, lo
+        if s == 2:
+            return (zh + 2) % Z, 1 - lo
+        return (zh + Z - 1 + 2 * lo) % Z, s // 2
+
+    def comes_from(s, b):
+        from_zh, from_lo = z_of_slot(s)
+        return {"grp": x * LO + from_lo, "ref": (from_zh * Y + (y + Y - b) % Y) * 2 + core}
+
+    def returns_to(s, b):
+        return comes_from(s, b), (0, 1 + 2 * lo, 2, 1 + 2 * lo)[s] * Y + b
 
     def remote(src, dst, send_sem, recv_sem, **where):
         return pltpu.make_async_remote_copy(
@@ -87,7 +102,7 @@
 
     barrier = pltpu.get_barrier_semaphore()
     for a, b in far_first:
-        pl.semaphore_signal(barrier, inc=1, device_id={"ref": behind(a, b)}, device_id_type=MESH)
+        pl.semaphore_signal(barrier, inc=1, device_id=comes_from(a, b), device_id_type=MESH)
     for j in range(1, n_grp):
         pl.semaphore_signal(barrier, inc=1, device_id={"grp": (mine + j) % n_grp}, device_id_type=MESH)
     pl.semaphore_signal(barrier, inc=1, device_id={"ref": mate}, device_id_type=MESH)
@@ -116,7 +131,8 @@
     pl.semaphore_wait(barrier, chips - 1 + n_grp - 1 + 1)
 
     for a, b in far_first:
-        remote(p_ref, rows.at[a * Y + b], row_send, row_recv.at[a], ref=ahead(a, b)).start()
+        where, slot = goes_to(a, b)
+        remote(p_ref, rows.at[slot], row_send, row_recv.at[slot // Y], **where).start()
     for j in range(1, n_grp):
         remote(p_ref, cols.at[j], col_send, col_recv, grp=(mine + j) % n_grp).start()
 
@@ -127,30 +143,43 @@
         n = Y - 1 if a == 0 else Y
         slots(rows, 0, n, row_send, row_recv.at[a]).wait_recv()
         remote(rows.at[pl.ds(a * Y, Y)], rows.at[pl.ds(chips + a * Y, Y)], fwd_send, fwd_recv, ref=mate).start()
-        if a == 0:
-            slots(cols, 0, n_grp - 1, col_send, col_recv).wait_recv()
-            remote(cols.at[pl.ds(0, n_grp)], cols.at[pl.ds(n_grp, n_grp)], fwc_send, fwc_recv, ref=mate).start()
+    forward_rows = slots(rows, chips, chips, fwd_send, fwd_recv)
+    slots(cols, 0, n_grp - 1, col_send, col_recv).wait_recv()
+    remote(cols.at[pl.ds(0, n_grp)], cols.at[pl.ds(n_grp, n_grp)], fwc_send, fwc_recv, ref=mate).start()
     forward_cols = slots(cols, n_grp, n_grp, fwc_send, fwc_recv)
+
+    def prepare(start):
+        wide = rows[pl.ds(start, chips)].astype(jnp.float32).reshape(half, d)
+        pmat[pl.ds(start * part, half), :] = wide.astype(jnp.bfloat16)
+        square = jnp.sum(wide * wide, axis=1, keepdims=True)
+        n = Y * part
+        mean = jnp.sum(wide.reshape(Z, n, d), axis=1, keepdims=True) * (1.0 / n)
+        of_mean = jnp.sum(mean * mean, axis=2, keepdims=True)
+        of_rows = jnp.sum(square.reshape(Z, n, 1), axis=1, keepdims=True) * (1.0 / n)
+        noise = (of_rows - of_mean) * (1.0 / (n - 1))
+        return square * SCALE, mean * jnp.maximum(1.0 - noise / jnp.maximum(of_mean, 1e-30), 0.0)
+
+    def less_center(total, mass, center):
+        parted = total.reshape(Z, Y * part, d) - mass.reshape(Z, Y * part, 1) * center
+        return parted.reshape(half, d)
+
+    own_sq, own_center = prepare(0)
     forward_cols.wait_recv()
-
-    cwide = cols[...].astype(jnp.float32).reshape(2 * n_grp * part, d)
-    cmat = cwide.astype(jnp.bfloat16)
+    cmat = cols[...].astype(jnp.float32).reshape(2 * n_grp * part, d).astype(jnp.bfloat16)
     col_sq = lane_square_norms(cmat) * SCALE
     n_cols = 2 * n_grp * part
 
-    forward_rows = slots(rows, chips, chips, fwd_send, fwd_recv)
-    forward_rows.wait_recv()
-    wide = rows[...].astype(jnp.float32).reshape(2 * half, d)
-    pmat[...] = wide.astype(jnp.bfloat16)
-    row_sq = jnp.sum(wide * wide, axis=1, keepdims=True) * SCALE
-    center = jnp.sum(wide, axis=0, keepdims=True) * (1.0 / (2 * half))
-
     s = dot_nt(pmat[pl.ds(0, half), :], cmat)
     s = s * (2.0 * SCALE) - col_sq
-    r = lax.broadcasted_iota(jnp.int32, (half, n_cols), 0)
+    r = lax.broadcasted_iota(jnp.int32, (half, 1), 0)
     a, b = r // (Y * part), (r // part) % Y
-    row_id = mine * (2 * half) + (((zh + Z - a) % Z * Y + (y + Y - b) % Y) * 2 + core) * part + r % part
-    q = lax.broadcasted_iota(jnp.int32, (half, n_cols), 1)
+    row_base = jnp.zeros((half, 1), jnp.int32)
+    for n in range(Z):
+        from_zh, from_lo = z_of_slot(n)
+        base = (x * LO + from_lo) * (2 * half) + (from_zh * Y * 2 + core) * part
+        row_base = jnp.where(a == n, base, row_base)
+    row_id = row_base + ((y + Y - b) % Y) * (2 * part) + r % part
+    q = lax.broadcasted_iota(jnp.int32, (1, n_cols), 1)
     j = (q // part) % n_grp
     col_id = (
         (mine + n_grp - j) % n_grp * (2 * half)
@@ -162,13 +191,16 @@
     s_top = jnp.max(s, axis=1, keepdims=True)
     w = jnp.where(same, 0.0, jnp.exp2(s - s_top))
     s_mass = jnp.sum(w, axis=1, keepdims=True)
-    s_sum = jnp.dot(w.astype(jnp.bfloat16), cmat, preferred_element_type=jnp.float32) - s_mass * center
-    send_s[...] = s_sum.reshape(chips, part, d).astype(jnp.bfloat16)
+    s_sum = jnp.dot(w.astype(jnp.bfloat16), cmat, preferred_element_type=jnp.float32)
+    send_s[...] = less_center(s_sum, s_mass, own_center).reshape(chips, part, d).astype(jnp.bfloat16)
 
     for a, b in far_first:
-        k = a * Y + b
-        remote(send_s.at[k], recv_s.at[k], s_send, s_recv, ref=behind(a, b)).start()
+        where, slot = returns_to(a, b)
+        remote(send_s.at[a * Y + b], recv_s.at[slot], s_send, s_recv, **where).start()
     recv_s[0] = send_s[0]
+
+    forward_rows.wait_recv()
+    other_sq, other_center = prepare(chips)
 
     top = jnp.full((2 * half, LANES), -jnp.inf, jnp.float32)
     for j in range(chunks):
@@ -188,27 +220,29 @@
         else:
             acc[...] += term
     mass = jnp.sum(mass, axis=1, keepdims=True)
-    total = acc[...] - mass * center
-    top = top - row_sq
-
-    send_m[:, pl.ds(0, d)] = total[half:].astype(jnp.bfloat16)
-    send_m[:, pl.ds(d, LANES)] = stats_lanes(top[half:], mass[half:]).astype(jnp.bfloat16)
+    own_mass, other_mass = mass[:half], mass[half:]
+    own_top, other_top = top[:half] - own_sq, top[half:] - other_sq
+    own_total = less_center(acc[pl.ds(0, half), :], own_mass, own_center)
+    other_total = less_center(acc[pl.ds(half, half), :], other_mass, other_center)
+
+    send_m[:, pl.ds(0, d)] = other_total.astype(jnp.bfloat16)
+    send_m[:, pl.ds(d, LANES)] = stats_lanes(other_top, other_mass).astype(jnp.bfloat16)
     swap = remote(send_m, recv_m, m_send, m_recv, ref=mate)
     swap.start()
     swap.wait_recv()
     theirs = recv_m[:, pl.ds(0, d)].astype(jnp.float32)
     stats = recv_m[:, pl.ds(d, LANES)].astype(jnp.float32)
-    c_top = jnp.maximum(top[:half], stat(stats, 0))
-    ours_share, their_share = jnp.exp2(top[:half] - c_top), jnp.exp2(stat(stats, 0) - c_top)
-    c_mass = mass[:half] * ours_share + stat(stats, 1) * their_share
-    c_sum = total[:half] * ours_share + theirs * their_share
+    c_top = jnp.maximum(own_top, stat(stats, 0))
+    ours_share, their_share = jnp.exp2(own_top - c_top), jnp.exp2(stat(stats, 0) - c_top)
+    c_mass = own_mass * ours_share + stat(stats, 1) * their_share
+    c_sum = own_total * ours_share + theirs * their_share
     send_c[:, :, pl.ds(0, d)] = c_sum.reshape(chips, part, d).astype(jnp.bfloat16)
-    stats = stats_lanes(c_top, c_mass, s_top - row_sq[:half], s_mass)
+    stats = stats_lanes(c_top, c_mass, s_top - own_sq, s_mass)
     send_c[:, :, pl.ds(d, LANES)] = stats.reshape(chips, part, LANES).astype(jnp.bfloat16)
 
     for a, b in far_first:
-        k = a * Y + b
-        remote(send_c.at[k], recv_c.at[k], c_send, c_recv, ref=behind(a, b)).start()
+        where, slot = returns_to(a, b)
+        remote(send_c.at[a * Y + b], recv_c.at[slot], c_send, c_recv, **where).start()
     recv_c[0] = send_c[0]
 
     got_s = slots(recv_s, 0, chips - 1, s_send, s_recv)

time: 32.2 us -> 30.1 us (0.935)
  Pallas kernels: 30.4 us -> 28.6 us
    pallas_call x1, Pallas kernels: 30.4 us -> 28.6 us  [per_device(): pl.pallas_call(kernel, out_shape=jax.ShapeDtypeStruct((part, d), f32), in...]
where the time goes in v3:
time: 30.1 us; the launch traced here: 29.9 us
  Pallas kernels  28.6 us (95%)
  local copies, waits for them, and re-layouts  1.32 us (4%)
    pallas_call x1, Pallas kernels, per_device(): pl.pallas_call(kernel, out_shape=jax.ShapeDtypeStruct((part, d), f32), in...  28.6 us
    unnamed x1, local copies, waits for them, and re-layouts  1.32 us

profile of v3, /device:TPU:2, one launch (start us, length us, event | category | flops | bytes accessed | tf_op | source)
XLA Modules:
  0.0 29.9 jit_solution(664181834562314232)
XLA Ops:
  0.0 28.6 %mmd_step.1 = f32[8,512]{1,0:T(8,128)} custom-call(bf16[8,512]{1,0:T(8,128)(2,1)} %p_hbm.1, bf16[4096,512]{1,0:T(8,128)(2,1)} %samples_ref.1), custom_call_target="tpu_custom_call" | custom-call | tf_op jit(solution)/shard_map/mmd_step/pallas_call | solution.py:272
  28.6 1.3 %copy.4 = f32[8,512]{1,0:T(8,128)} copy(f32[8,512]{1,0:T(8,128)} %mmd_step.1) | data formatting | bytes 32768

commit v4 on v3

v4 whole, which is shorter than its diff:
```python
import functools
import math

import jax
import jax.numpy as jnp
from jax import lax
from jax.experimental import pallas as pl
from jax.experimental.pallas import tpu as pltpu
from jax.sharding import PartitionSpec as P

KERNEL_WIDTH = 16
STEP_SIZE = 8.0
MASKED = -1e30
SCALE = math.log2(math.e) / (2.0 * KERNEL_WIDTH)
MESH = pl.DeviceIdType.MESH
CHUNK = 512
LATE = 3
LANES = 128
VMEM_BYTES = 56 * 2**20
Z, Y, LO = 4, 4, 2


def packed(part, *columns):
    rows, n = columns[0].shape[0], len(columns)
    lane = lax.broadcasted_iota(jnp.int32, (rows, LANES), 1)
    row = lax.broadcasted_iota(jnp.int32, (rows, LANES), 0) % part
    line = jnp.zeros((rows, LANES), jnp.float32)
    for k, column in enumerate(columns):
        line = jnp.where(lane == row * n + k, column, line)
    return jnp.sum(line.reshape(rows // part, part, LANES), axis=1, keepdims=True)


def unpacked(lines, part, n):
    shape = (lines.shape[0], part, LANES)
    lane = lax.broadcasted_iota(jnp.int32, shape, 2)
    row = lax.broadcasted_iota(jnp.int32, shape, 1)
    wide = jnp.broadcast_to(lines, shape)
    return [
        jnp.sum(jnp.where(lane == row * n + k, wide, 0.0), axis=2, keepdims=True) for k in range(n)
    ]


def merged_mean(parts, top, mass):
    share = jnp.exp2(top - jnp.max(top, axis=0, keepdims=True))
    return jnp.sum(share * parts, axis=0) / jnp.sum(share * mass, axis=0)


def turned(values):
    across = values.T
    wide = across.astype(jnp.float32)
    return across, jnp.sum(wide * wide, axis=0, keepdims=True)


def dot(a, b):
    return jnp.dot(a, b, preferred_element_type=jnp.float32)


def kernel(
    p_hbm, samples_ref, out_ref,
    p_ref, smp, turn, rows, cols, pmat, ref_sq, scores, acc,
    send_c, recv_c, send_s, recv_s, send_t, recv_t,
    load_sem, p_sem, row_send, row_recv, col_send, col_recv, smp_send, smp_recv,
    c_send, c_recv, s_send, s_recv, t_send, t_recv,
):
    n_grp = lax.axis_size("grp")
    me, mine = lax.axis_index("ref"), lax.axis_index("grp")
    core, y, zh = me % 2, (me // 2) % Y, me // (2 * Y)
    mate = me + 1 - 2 * core
    part, d = p_ref.shape
    chips = Z * Y
    half = chips * part
    chunks = smp.shape[0] // 2
    far_first = [(a, b) for a in (2, 1, 3, 0) for b in (2, 1, 3, 0) if (a, b) != (0, 0)]

    lo, x = mine % LO, mine // LO

    def goes_to(a, b):
        to_lo = (lo, 0, 1 - lo, 1)[a]
        where = {"grp": x * LO + to_lo, "ref": (((zh + a) % Z) * Y + (y + b) % Y) * 2 + core}
        return where, (0, 1 + 2 * lo, 2, 1 + 2 * lo)[a] * Y + b

    def z_of_slot(s):
        if s == 0:
            return zh, lo
        if s == 2:
            return (zh + 2) % Z, 1 - lo
        return (zh + Z - 1 + 2 * lo) % Z, s // 2

    def comes_from(s, b):
        from_zh, from_lo = z_of_slot(s)
        return {"grp": x * LO + from_lo, "ref": (from_zh * Y + (y + Y - b) % Y) * 2 + core}

    def returns_to(s, b):
        return comes_from(s, b), (0, 1 + 2 * lo, 2, 1 + 2 * lo)[s] * Y + b

    def remote(src, dst, send_sem, recv_sem, **where):
        return pltpu.make_async_remote_copy(
            src, dst, send_sem, recv_sem, device_id=where, device_id_type=MESH
        )

    barrier = pltpu.get_barrier_semaphore()
    for a, b in far_first:
        pl.semaphore_signal(barrier, inc=1, device_id=comes_from(a, b), device_id_type=MESH)
    for j in range(1, n_grp):
        pl.semaphore_signal(barrier, inc=1, device_id={"grp": (mine + j) % n_grp}, device_id_type=MESH)
    for j in range(n_grp):
        where = {"grp": (mine + j) % n_grp, "ref": mate}
        pl.semaphore_signal(barrier, inc=1, device_id=where, device_id_type=MESH)

    load_p = pltpu.make_async_copy(p_hbm, p_ref, p_sem)
    load_p.start()

    def load(j):
        return pltpu.make_async_copy(
            samples_ref.at[pl.ds(j * CHUNK, CHUNK)], smp.at[j], load_sem.at[j]
        )

    for j in range(chunks):
        load(j).start()

    load_p.wait()
    rows[0] = p_ref[...]
    cols[0] = p_ref[...]

    def take(j):
        across, square = turned(smp[j])
        turn[j] = across
        ref_sq[j] = square * SCALE

    def take_own(j, c):
        load(j).wait()
        take(j)
        return c

    pl.semaphore_wait(barrier, chips - 1 + n_grp - 1 + n_grp)

    for a, b in far_first:
        where, slot = goes_to(a, b)
        remote(p_ref, rows.at[slot], row_send, row_recv, **where).start()

    for j in range(1, n_grp):
        remote(p_ref, cols.at[j], col_send, col_recv, grp=(mine + j) % n_grp).start()
    for j in range(n_grp):
        where = {"grp": (mine + j) % n_grp, "ref": mate}
        remote(p_ref, cols.at[n_grp + j], col_send, col_recv, **where).start()

    def pass_on(j):
        return remote(smp.at[j], smp.at[chunks + j], smp_send, smp_recv.at[j], ref=mate)

    def take_other(j, c):
        pass_on(j).wait_recv()
        take(chunks + j)
        return c


    def pass_first(j, c):
        load(j).wait()
        pass_on(j).start()
        return c

    for j in range(0):
        pass_on(j).start()
    lax.fori_loop(0, chunks, pass_first, 0)

    def take_rest(j, c):
        take(j)
        return c

    lax.fori_loop(0, chunks, take_rest, 0)
    lax.fori_loop(0, chunks - LATE, take_other, 0)

    def slots(buf, start, n, send_sem, recv_sem):
        return remote(buf.at[pl.ds(start, n)], buf.at[pl.ds(start, n)], send_sem, recv_sem, ref=mate)

    got_rows = slots(rows, 0, chips - 1, row_send, row_recv)
    got_rows.wait_recv()
    wide = rows[...].astype(jnp.float32).reshape(half, d)
    pmat[...] = wide.astype(jnp.bfloat16)
    row_sq = jnp.sum(wide * wide, axis=1, keepdims=True)
    n = Y * part
    center = jnp.sum(wide.reshape(Z, n, d), axis=1, keepdims=True) * (1.0 / n)
    of_mean = jnp.sum(center * center, axis=2, keepdims=True)
    of_rows = jnp.sum(row_sq.reshape(Z, n, 1), axis=1, keepdims=True) * (1.0 / n)
    noise = (of_rows - of_mean) * (1.0 / (n - 1))
    center = center * jnp.maximum(1.0 - noise / jnp.maximum(of_mean, 1e-30), 0.0)
    row_sq = row_sq * SCALE

    def less_center(total, mass):
        parted = total.reshape(Z, Y * part, d) - mass.reshape(Z, Y * part, 1) * center
        return parted.reshape(half, d)

    got_cols = slots(cols, 0, 2 * n_grp - 1, col_send, col_recv)
    got_cols.wait_recv()
    cmat = cols[...].astype(jnp.float32).reshape(2 * n_grp * part, d).astype(jnp.bfloat16)
    cturn, col_sq = turned(cmat)
    n_cols = 2 * n_grp * part

    s = (dot(pmat[...], cturn) * 2.0 - col_sq) * SCALE
    r = lax.broadcasted_iota(jnp.int32, (half, 1), 0)
    a, b = r // (Y * part), (r // part) % Y
    row_base = jnp.zeros((half, 1), jnp.int32)
    for n in range(Z):
        from_zh, from_lo = z_of_slot(n)
        base = (x * LO + from_lo) * (2 * half) + (from_zh * Y * 2 + core) * part
        row_base = jnp.where(a == n, base, row_base)
    row_id = row_base + ((y + Y - b) % Y) * (2 * part) + r % part
    q = lax.broadcasted_iota(jnp.int32, (1, n_cols), 1)
    j = (q // part) % n_grp
    col_id = (
        (mine + n_grp - j) % n_grp * (2 * half)
        + jnp.where(q < n_grp * part, me, mate) * part
        + q % part
    )
    same = row_id == col_id
    s = jnp.where(same, MASKED, s)
    s_top = jnp.max(s, axis=1, keepdims=True)
    w = jnp.where(same, 0.0, jnp.exp2(s - s_top))
    s_mass = jnp.sum(w, axis=1, keepdims=True)
    s_sum = dot(w.astype(jnp.bfloat16), cmat)
    send_s[...] = less_center(s_sum, s_mass).reshape(chips, part, d).astype(jnp.bfloat16)

    for a, b in far_first:
        where, slot = returns_to(a, b)
        remote(send_s.at[a * Y + b], recv_s.at[slot], s_send, s_recv, **where).start()
    recv_s[0] = send_s[0]

    top = jnp.full((half, LANES), -jnp.inf, jnp.float32)
    for j in range(2 * chunks):
        if j >= 2 * chunks - LATE:
            pass_on(j - chunks).wait_recv()
            take(j)
        s = dot(pmat[...], turn[j]) * (2.0 * SCALE) - ref_sq[j]
        scores[j] = s
        for at in range(0, CHUNK, LANES):
            top = jnp.maximum(top, s[:, at : at + LANES])
    top = jnp.max(top, axis=1, keepdims=True)
    mass = jnp.zeros((half, LANES), jnp.float32)
    for j in range(2 * chunks):
        w = jnp.exp2(scores[j] - top)
        for at in range(0, CHUNK, LANES):
            mass = mass + w[:, at : at + LANES]
        term = dot(w.astype(jnp.bfloat16), smp[j])
        if j == 0:
            acc[...] = term
        else:
            acc[...] += term
    mass = jnp.sum(mass, axis=1, keepdims=True)
    send_t[...] = packed(part, top - row_sq, mass, s_top - row_sq, s_mass)
    for a, b in far_first:
        where, slot = returns_to(a, b)
        remote(send_t.at[a * Y + b], recv_t.at[slot], t_send, t_recv, **where).start()
    recv_t[0] = send_t[0]
    total = less_center(acc[...], mass)
    send_c[...] = total.reshape(chips, part, d).astype(jnp.bfloat16)

    for a, b in far_first:
        where, slot = returns_to(a, b)
        remote(send_c.at[a * Y + b], recv_c.at[slot], c_send, c_recv, **where).start()
    recv_c[0] = send_c[0]

    got_s = slots(recv_s, 0, chips - 1, s_send, s_recv)
    got_c = slots(recv_c, 0, chips - 1, c_send, c_recv)
    got_t = slots(recv_t, 0, chips - 1, t_send, t_recv)
    got_s.wait_recv()
    got_t.wait_recv()
    c_top, c_mass, s_top, s_mass = unpacked(recv_t[...], part, 4)
    own = merged_mean(recv_s[...].astype(jnp.float32), s_top, s_mass)
    got_c.wait_recv()
    cross = merged_mean(recv_c[...].astype(jnp.float32), c_top, c_mass)
    out_ref[...] = p_ref[...].astype(jnp.float32) + STEP_SIZE * (cross - own)
    got_rows.wait_send()
    got_cols.wait_send()
    slots(smp, 0, chunks, smp_send, smp_recv.at[0]).wait_send()
    got_s.wait_send()
    got_c.wait_send()
    got_t.wait_send()


def per_device(n_ref, n_grp, particles, samples):
    part, d = particles.shape
    refs = samples.shape[0]
    chips, chunks = n_ref // 2, refs // CHUNK
    half = chips * part
    dma = pltpu.SemaphoreType.DMA
    bf16, f32 = jnp.bfloat16, jnp.float32
    return pl.pallas_call(
        kernel,
        out_shape=pltpu.VMEM((part, d), f32),
        in_specs=[pl.BlockSpec(memory_space=pl.ANY)] * 2,
        out_specs=pl.BlockSpec(memory_space=pltpu.VMEM),
        scratch_shapes=[
            pltpu.VMEM((part, d), bf16),
            pltpu.VMEM((2 * chunks, CHUNK, d), bf16),
            pltpu.VMEM((2 * chunks, d, CHUNK), bf16),
            pltpu.VMEM((chips, part, d), bf16),
            pltpu.VMEM((2 * n_grp, part, d), bf16),
            pltpu.VMEM((half, d), bf16),
            pltpu.VMEM((2 * chunks, 1, CHUNK), f32),
            pltpu.VMEM((2 * chunks, half, CHUNK), f32),
            pltpu.VMEM((half, d), f32),
            pltpu.VMEM((chips, part, d), bf16),
            pltpu.VMEM((chips, part, d), bf16),
            pltpu.VMEM((chips, part, d), bf16),
            pltpu.VMEM((chips, part, d), bf16),
            pltpu.VMEM((chips, 1, LANES), f32),
            pltpu.VMEM((chips, 1, LANES), f32),
            dma((chunks,)), dma, dma, dma, dma, dma, dma, dma((chunks,)),
            dma, dma, dma, dma, dma, dma,
        ],
        compiler_params=pltpu.CompilerParams(
            collective_id=0, has_side_effects=True, vmem_limit_bytes=VMEM_BYTES
        ),
        name="mmd_step",
    )(particles, samples)


def solution(mesh):
    step = functools.partial(per_device, mesh.shape["ref"], mesh.shape["grp"])
    return jax.shard_map(
        step,
        mesh=mesh,
        in_specs=(P(("grp", "ref"), None), P("ref", None)),
        out_specs=P(("grp", "ref"), None),
        check_vma=False,
    )
```

time: 30.1 us -> 26.4 us (0.88)
  Pallas kernels: 28.6 us -> 25.7 us
  local copies, waits for them, and re-layouts: 1.32 us -> 0.61 us
    pallas_call x1, Pallas kernels: 28.6 us -> 25.7 us  [per_device(): pl.pallas_call(kernel, out_shape=pltpu.VMEM((part, d), f32), in_specs=[pl...]
    unnamed x1, local copies, waits for them, and re-layouts: 1.32 us -> 0.61 us
where the time goes in v4:
time: 26.4 us; the launch traced here: 26.3 us
  Pallas kernels  25.7 us (97%)
  local copies, waits for them, and re-layouts  0.61 us (2%)
    pallas_call x1, Pallas kernels, per_device(): pl.pallas_call(kernel, out_shape=pltpu.VMEM((part, d), f32), in_specs=[pl...  25.7 us
    unnamed x1, local copies, waits for them, and re-layouts  0.61 us

profile of v4, /device:TPU:2, one launch (start us, length us, event | category | flops | bytes accessed | tf_op | source)
XLA Modules:
  0.0 26.3 jit_solution(7661377619562398111)
XLA Ops:
  0.0 25.7 %mmd_step.1 = f32[8,512]{1,0:T(8,128)S(1)} custom-call(bf16[8,512]{1,0:T(8,128)(2,1)} %p_hbm.1, bf16[4096,512]{1,0:T(8,128)(2,1)} %samples_ref.1), custom_call_target="tpu_custom_call" | custom-call | tf_op jit(solution)/shard_map/mmd_step/pallas_call | solution.py:286
  25.7 0.6 %copy.4 = f32[8,512]{1,0:T(8,128)} copy(f32[8,512]{1,0:T(8,128)S(1)} %mmd_step.1) | data formatting | bytes 32768

commit v5 on v4

--- a/solution.py
+++ b/solution.py
@@ -40,9 +40,9 @@
     ]
 
 
-def merged_mean(parts, top, mass):
+def shares(top, mass):
     share = jnp.exp2(top - jnp.max(top, axis=0, keepdims=True))
-    return jnp.sum(share * parts, axis=0) / jnp.sum(share * mass, axis=0)
+    return share / jnp.sum(share * mass, axis=0, keepdims=True)
 
 
 def turned(values):
@@ -219,13 +219,14 @@
     s_sum = dot(w.astype(jnp.bfloat16), cmat)
     send_s[...] = less_center(s_sum, s_mass).reshape(chips, part, d).astype(jnp.bfloat16)
 
-    for a, b in far_first:
-        where, slot = returns_to(a, b)
-        remote(send_s.at[a * Y + b], recv_s.at[slot], s_send, s_recv, **where).start()
-    recv_s[0] = send_s[0]
 
     top = jnp.full((half, LANES), -jnp.inf, jnp.float32)
     for j in range(2 * chunks):
+        if j == 2 * chunks - LATE:
+            for a, b in far_first:
+                where, slot = returns_to(a, b)
+                remote(send_s.at[a * Y + b], recv_s.at[slot], s_send, s_recv, **where).start()
+            recv_s[0] = send_s[0]
         if j >= 2 * chunks - LATE:
             pass_on(j - chunks).wait_recv()
             take(j)
@@ -264,10 +265,14 @@
     got_s.wait_recv()
     got_t.wait_recv()
     c_top, c_mass, s_top, s_mass = unpacked(recv_t[...], part, 4)
-    own = merged_mean(recv_s[...].astype(jnp.float32), s_top, s_mass)
+    wide = p_ref[...].astype(jnp.float32)
+    s_share = shares(s_top, s_mass) * STEP_SIZE
+    c_share = jnp.broadcast_to(shares(c_top, c_mass) * STEP_SIZE, (chips, part, LANES))
+    out_ref[...] = wide - jnp.sum(s_share * recv_s[...].astype(jnp.float32), axis=0)
     got_c.wait_recv()
-    cross = merged_mean(recv_c[...].astype(jnp.float32), c_top, c_mass)
-    out_ref[...] = p_ref[...].astype(jnp.float32) + STEP_SIZE * (cross - own)
+    for at in range(0, d, LANES):
+        lanes = pl.ds(at, LANES)
+        out_ref[:, lanes] += jnp.sum(c_share * recv_c[:, :, lanes].astype(jnp.float32), axis=0)
     got_rows.wait_send()
     got_cols.wait_send()
     slots(smp, 0, chunks, smp_send, smp_recv.at[0]).wait_send()

time: 26.4 us -> 26.1 us (0.989)
  Pallas kernels: 25.7 us -> 25.4 us
    pallas_call x1, Pallas kernels: 25.7 us -> 25.4 us  [per_device(): pl.pallas_call(kernel, out_shape=pltpu.VMEM((part, d), f32), in_specs=[pl...]
where the time goes in v5:
time: 26.1 us; the launch traced here: 26 us
  Pallas kernels  25.4 us (97%)
  local copies, waits for them, and re-layouts  0.61 us (2%)
    pallas_call x1, Pallas kernels, per_device(): pl.pallas_call(kernel, out_shape=pltpu.VMEM((part, d), f32), in_specs=[pl...  25.4 us
    unnamed x1, local copies, waits for them, and re-layouts  0.61 us

profile of v5, /device:TPU:2, one launch (start us, length us, event | category | flops | bytes accessed | tf_op | source)
XLA Modules:
  0.0 26.0 jit_solution(11141541496357955665)
XLA Ops:
  0.0 25.4 %mmd_step.1 = f32[8,512]{1,0:T(8,128)S(1)} custom-call(bf16[8,512]{1,0:T(8,128)(2,1)} %p_hbm.1, bf16[4096,512]{1,0:T(8,128)(2,1)} %samples_ref.1), custom_call_target="tpu_custom_call" | custom-call | tf_op jit(solution)/shard_map/mmd_step/pallas_call | solution.py:291
  25.4 0.6 %copy.4 = f32[8,512]{1,0:T(8,128)} copy(f32[8,512]{1,0:T(8,128)S(1)} %mmd_step.1) | data formatting | bytes 32768

commit v6 on v5

--- a/solution.py
+++ b/solution.py
@@ -13,8 +13,8 @@
 MASKED = -1e30
 SCALE = math.log2(math.e) / (2.0 * KERNEL_WIDTH)
 MESH = pl.DeviceIdType.MESH
-CHUNK = 512
-LATE = 3
+CHUNK = 1024
+LATE = 1
 LANES = 128
 VMEM_BYTES = 56 * 2**20
 Z, Y, LO = 4, 4, 2

time: 26.1 us -> 26.5 us (1.015)
  the two profiles are of different devices: /device:TPU:2 before, /device:TPU:32 now
where the time goes in v6:
time: 26.5 us; the launch traced here: 26.4 us
  Pallas kernels  25.8 us (97%)
  local copies, waits for them, and re-layouts  0.61 us (2%)
    pallas_call x1, Pallas kernels, per_device(): pl.pallas_call(kernel, out_shape=pltpu.VMEM((part, d), f32), in_specs=[pl...  25.8 us
    unnamed x1, local copies, waits for them, and re-layouts  0.61 us

profile of v6, /device:TPU:32, one launch (start us, length us, event | category | flops | bytes accessed | tf_op | source)
XLA Modules:
  0.0 26.4 jit_solution(1780359986801859076)
XLA Ops:
  0.0 25.8 %mmd_step.1 = f32[8,512]{1,0:T(8,128)S(1)} custom-call(bf16[8,512]{1,0:T(8,128)(2,1)} %p_hbm.1, bf16[4096,512]{1,0:T(8,128)(2,1)} %samples_ref.1), custom_call_target="tpu_custom_call" | custom-call | tf_op jit(solution)/shard_map/mmd_step/pallas_call | solution.py:291
  25.8 0.6 %copy.4 = f32[8,512]{1,0:T(8,128)} copy(f32[8,512]{1,0:T(8,128)S(1)} %mmd_step.1) | data formatting | bytes 32768

commit v7 on v5

--- a/solution.py
+++ b/solution.py
@@ -172,30 +172,7 @@
     def slots(buf, start, n, send_sem, recv_sem):
         return remote(buf.at[pl.ds(start, n)], buf.at[pl.ds(start, n)], send_sem, recv_sem, ref=mate)
 
-    got_rows = slots(rows, 0, chips - 1, row_send, row_recv)
-    got_rows.wait_recv()
-    wide = rows[...].astype(jnp.float32).reshape(half, d)
-    pmat[...] = wide.astype(jnp.bfloat16)
-    row_sq = jnp.sum(wide * wide, axis=1, keepdims=True)
-    n = Y * part
-    center = jnp.sum(wide.reshape(Z, n, d), axis=1, keepdims=True) * (1.0 / n)
-    of_mean = jnp.sum(center * center, axis=2, keepdims=True)
-    of_rows = jnp.sum(row_sq.reshape(Z, n, 1), axis=1, keepdims=True) * (1.0 / n)
-    noise = (of_rows - of_mean) * (1.0 / (n - 1))
-    center = center * jnp.maximum(1.0 - noise / jnp.maximum(of_mean, 1e-30), 0.0)
-    row_sq = row_sq * SCALE
-
-    def less_center(total, mass):
-        parted = total.reshape(Z, Y * part, d) - mass.reshape(Z, Y * part, 1) * center
-        return parted.reshape(half, d)
-
-    got_cols = slots(cols, 0, 2 * n_grp - 1, col_send, col_recv)
-    got_cols.wait_recv()
-    cmat = cols[...].astype(jnp.float32).reshape(2 * n_grp * part, d).astype(jnp.bfloat16)
-    cturn, col_sq = turned(cmat)
     n_cols = 2 * n_grp * part
-
-    s = (dot(pmat[...], cturn) * 2.0 - col_sq) * SCALE
     r = lax.broadcasted_iota(jnp.int32, (half, 1), 0)
     a, b = r // (Y * part), (r // part) % Y
     row_base = jnp.zeros((half, 1), jnp.int32)
@@ -212,6 +189,30 @@
         + q % part
     )
     same = row_id == col_id
+
+    got_rows = slots(rows, 0, chips - 1, row_send, row_recv)
+    got_rows.wait_recv()
+    wide = rows[...].astype(jnp.float32).reshape(half, d)
+    pmat[...] = wide.astype(jnp.bfloat16)
+    row_sq = jnp.sum(wide * wide, axis=1, keepdims=True)
+    n = Y * part
+    center = jnp.sum(wide.reshape(Z, n, d), axis=1, keepdims=True) * (1.0 / n)
+    of_mean = jnp.sum(center * center, axis=2, keepdims=True)
+    of_rows = jnp.sum(row_sq.reshape(Z, n, 1), axis=1, keepdims=True) * (1.0 / n)
+    noise = (of_rows - of_mean) * (1.0 / (n - 1))
+    center = center * jnp.maximum(1.0 - noise / jnp.maximum(of_mean, 1e-30), 0.0)
+    row_sq = row_sq * SCALE
+
+    def less_center(total, mass):
+        parted = total.reshape(Z, Y * part, d) - mass.reshape(Z, Y * part, 1) * center
+        return parted.reshape(half, d)
+
+    got_cols = slots(cols, 0, 2 * n_grp - 1, col_send, col_recv)
+    got_cols.wait_recv()
+    cmat = cols[...].astype(jnp.float32).reshape(2 * n_grp * part, d).astype(jnp.bfloat16)
+    cturn, col_sq = turned(cmat)
+
+    s = (dot(pmat[...], cturn) * 2.0 - col_sq) * SCALE
     s = jnp.where(same, MASKED, s)
     s_top = jnp.max(s, axis=1, keepdims=True)
     w = jnp.where(same, 0.0, jnp.exp2(s - s_top))

time: 26.1 us -> 26.1 us (level)
  no operation moved by 1% of the time
where the time goes in v7:
time: 26.1 us; the launch traced here: 26 us
  Pallas kernels  25.4 us (97%)
  local copies, waits for them, and re-layouts  0.61 us (2%)
    pallas_call x1, Pallas kernels, per_device(): pl.pallas_call(kernel, out_shape=pltpu.VMEM((part, d), f32), in_specs=[pl...  25.4 us
    unnamed x1, local copies, waits for them, and re-layouts  0.61 us

profile of v7, /device:TPU:2, one launch (start us, length us, event | category | flops | bytes accessed | tf_op | source)
XLA Modules:
  0.0 26.0 jit_solution(4933262814535389241)
XLA Ops:
  0.0 25.4 %mmd_step.1 = f32[8,512]{1,0:T(8,128)S(1)} custom-call(bf16[8,512]{1,0:T(8,128)(2,1)} %p_hbm.1, bf16[4096,512]{1,0:T(8,128)(2,1)} %samples_ref.1), custom_call_target="tpu_custom_call" | custom-call | tf_op jit(solution)/shard_map/mmd_step/pallas_call | solution.py:292
  25.4 0.6 %copy.4 = f32[8,512]{1,0:T(8,128)} copy(f32[8,512]{1,0:T(8,128)S(1)} %mmd_step.1) | data formatting | bytes 32768
